TPU v7x, 32 devices: a whole 2x2x4 slice. The times are simulated.
32 devices in a mesh: grp: 2 (over y), tok: 4 (over z), sec: 2 (over core), ch: 2 (over x).
Axes of the slice: x: 2, y: 2, z: 4, core: 2. Of those that a mesh axis runs over, the one named last changes fastest.
Arguments:
- features: bfloat16 [4096, 2048], P('ch', ('grp', 'tok', 'sec')), parts along dimension 1, may hold values from -6 to 6
- gate_one: bfloat16 [4096, 2048], P('ch', ('grp', 'tok', 'sec')), parts along dimension 1, may hold values from -6 to 6
- taps_one: bfloat16 [4096, 128], P('ch'), may hold values from -0.5 to 0.5
- long_filter: bfloat16 [4096, 1024], P('ch', ('tok', 'sec')), may hold values from -0.1875 to 0.1875
- skip_gain: float32 [4096], P('ch'), may hold values from 0.5 to 1.5
- taps_two: bfloat16 [4096, 128], P('ch'), may hold values from -0.5 to 0.5
- gate_two: bfloat16 [4096, 2048], P('ch', ('grp', 'tok', 'sec')), parts along dimension 1, may hold values from -6 to 6
Outputs:
- mixed_out: bfloat16 [4096, 2048], P('ch', ('grp', 'tok', 'sec')), parts along dimension 1
There are 2 independent parts, one for each index of `grp`. A program takes and returns all parts, laid end to end along the dimension named above; an argument that names none is the same for every part. Nothing has to cross between parts.
All inputs are finite; a program needn't handle non-finite values.
Results may differ from a plain program's by a relative error of at most 0.0057.
Values may be sent and summed in bfloat16 or wider, within the bound.
No kernel may reach another device: no remote copies, remote signals or barrier semaphores. Data moves between devices by JAX's collectives and lax.ppermute only.
A program may use at most 192 MiB of HBM per device.

v0:
```python
import math
import jax
import jax.numpy as jnp
from jax import lax
from jax.sharding import PartitionSpec as P


def passed_along(array, axis, by):
    length = lax.axis_size(axis)
    pairs = [(i, i + by) for i in range(length) if 0 <= i + by < length]
    return lax.ppermute(array, axis, pairs)


def depthwise(padded, kernel_taps):
    tap_count = kernel_taps.shape[1]
    length = padded.shape[1] - (tap_count - 1)
    group_size = 16
    total = jnp.zeros((padded.shape[0], length), jnp.float32)
    for first in range(0, tap_count, group_size):
        last = min(first + group_size, tap_count)
        stacked = jnp.stack(
            [padded[:, tap_count - 1 - k : tap_count - 1 - k + length] for k in range(first, last)],
            axis=1,
        )
        total = total + jnp.einsum(
            "cgl,cg->cl", stacked, kernel_taps[:, first:last], preferred_element_type=jnp.float32
        )
    return total


def angle_table(rows_count, cols_count, period):
    row_index = jnp.arange(rows_count, dtype=jnp.int32)[:, None]
    col_index = jnp.arange(cols_count, dtype=jnp.int32)[None, :]
    phase = (row_index * col_index % period).astype(jnp.float32) * (2.0 * math.pi / period)
    return (jnp.cos(phase), jnp.sin(phase))


def contract(form, left, right):
    return jnp.einsum(form, left, right, precision=lax.Precision.HIGHEST)


def forward_spectrum(signal, outer, inner, total):
    half_outer = outer // 2
    cos_first, sin_first = angle_table(half_outer, outer, outer)
    turn_cos, turn_sin = angle_table(outer, inner, total)
    cos_inner, sin_inner = angle_table(inner, inner, inner)
    shaped = signal.reshape(signal.shape[0], half_outer, inner)
    real_a = contract("cmn,mk->ckn", shaped, cos_first)
    imag_a = -contract("cmn,mk->ckn", shaped, sin_first)
    real_b = real_a * turn_cos + imag_a * turn_sin
    imag_b = imag_a * turn_cos - real_a * turn_sin
    real_c = contract("ckn,nj->cjk", real_b, cos_inner) + contract("ckn,nj->cjk", imag_b, sin_inner)
    imag_c = contract("ckn,nj->cjk", imag_b, cos_inner) - contract("ckn,nj->cjk", real_b, sin_inner)
    return (real_c, imag_c)


def inverse_spectrum(real_y, imag_y, outer, inner, total):
    half_outer = outer // 2
    cos_inner, sin_inner = angle_table(inner, inner, inner)
    turn_cos, turn_sin = angle_table(outer, inner, total)
    cos_last, sin_last = angle_table(outer, half_outer, outer)
    real_c = contract("cjk,jn->ckn", real_y, cos_inner) - contract("cjk,jn->ckn", imag_y, sin_inner)
    imag_c = contract("cjk,jn->ckn", imag_y, cos_inner) + contract("cjk,jn->ckn", real_y, sin_inner)
    real_d = real_c * turn_cos - imag_c * turn_sin
    imag_d = imag_c * turn_cos + real_c * turn_sin
    result = contract("ckn,km->cmn", real_d, cos_last) - contract("ckn,km->cmn", imag_d, sin_last)
    return (result / total).reshape(real_y.shape[0], half_outer * inner)


def on_device(features, gate_one, taps_one, long_filter, skip_gain, taps_two, gate_two):
    shards = lax.axis_size(("tok", "sec"))
    channels, block_len = features.shape
    narrow = channels // shards
    seq_len = block_len * shards
    rim_width = taps_one.shape[1] - 1
    total = 2 * seq_len
    inner = math.gcd(seq_len, 128)
    outer = total // inner
    filter_rows = lax.all_to_all(
        long_filter[:, None, :], ("tok", "sec"), split_axis=0, concat_axis=1, tiled=True
    ).reshape(narrow, seq_len)
    rim_rows = passed_along(features[:, block_len - rim_width :], ("tok", "sec"), 1)
    first_conv = depthwise(jnp.concatenate([rim_rows, features], axis=1), taps_one)
    mixed_one = (first_conv * gate_one).astype(jnp.bfloat16)
    channel_rows = lax.all_to_all(
        mixed_one[:, None, :], ("tok", "sec"), split_axis=0, concat_axis=1, tiled=True
    )
    channel_rows = channel_rows.reshape(narrow, seq_len).astype(jnp.float32)
    filter_real, filter_imag = forward_spectrum(
        filter_rows.astype(jnp.float32), outer, inner, total
    )
    signal_real, signal_imag = forward_spectrum(channel_rows, outer, inner, total)
    product_real = signal_real * filter_real - signal_imag * filter_imag
    product_imag = signal_real * filter_imag + signal_imag * filter_real
    conv_rows = inverse_spectrum(product_real, product_imag, outer, inner, total)
    skip_local = lax.dynamic_slice_in_dim(
        skip_gain, lax.axis_index(("tok", "sec")) * narrow, narrow
    )
    long_out = (conv_rows + skip_local[:, None] * channel_rows).astype(jnp.bfloat16)
    long_blocks = long_out.reshape(narrow, shards, block_len)
    tail_rows = jnp.concatenate(
        [
            jnp.zeros((narrow, 1, rim_width), jnp.bfloat16),
            long_blocks[:, :-1, block_len - rim_width :],
        ],
        axis=1,
    )
    windows = jnp.concatenate([tail_rows, long_blocks], axis=2)
    padded = lax.all_to_all(
        windows, ("tok", "sec"), split_axis=1, concat_axis=0, tiled=True
    ).reshape(channels, block_len + rim_width)
    second_conv = depthwise(padded, taps_two)
    return (second_conv * gate_two).astype(jnp.bfloat16)


def solution(mesh):
    in_specs = (
        P("ch", ("grp", "tok", "sec")),
        P("ch", ("grp", "tok", "sec")),
        P("ch", None),
        P("ch", ("tok", "sec")),
        P("ch"),
        P("ch", None),
        P("ch", ("grp", "tok", "sec")),
    )
    out_specs = P("ch", ("grp", "tok", "sec"))
    return jax.shard_map(
        on_device, mesh=mesh, in_specs=in_specs, out_specs=out_specs, check_vma=False
    )
```

profile of v0, /device:TPU:0, one launch (start us, length us, event | category | flops | bytes accessed | tf_op | source)
XLA Modules:
  0.0 428.6 jit_solution(18028862349489927458)
XLA Ops:
  8.2 6.1 %all-to-all-start.1 = ((bf16[8,2,16384]{2,1,0:T(2,128)(2,1)}), bf16[8,2,16384]{2,1,0:T(2,128)(2,1)S(1)}, u32[]{:S(2)}, u32[]{:S(2)}) async-start(bf16[8,2,16384]{2,1,0:T(2,128)(2,1)} %reshape.112), calls=%async_computation.1 | async-start | bytes 1048576 | tf_op jit(solution)/shard_map/all_to_all | solution.py:79
  14.3 5.7 %slice_bitcast_fusion.142 = (bf16[2048,16,1]{1,0,2:T(8,128)(2,1)S(1)}, bf16[2048,16,1]{1,0,2:T(8,128)(2,1)}, bf16[2048,16,1]{1,0,2:T(8,128)(2,1)}, bf16[2048,16,...) fusion(bf16[2048,128]{1,0:T(8,128)(2,1)} %param.9), kind=kLoop, calls=%fused_computation.1013 | loop fusion | bytes 1048576 | tf_op jit(solution)/shard_map/slice | solution.py:26
  28.0 3.2 copy-done.13
  31.2 3.7 constant_dynamic-update-slice_fusion.16
  110.7 8.7 %fusion.16 = f32[2048,1,128]{2,1,0:T(1,128)S(1)} fusion(bf16[2048,16,128]{2,0,1:T(8,128)(2,1)} %constant_dynamic-update-slice_fusion.112, bf16[2048,16,1]{1,0,2:T(8,128)(2,1)S(1)} %get-tuple-element.191), kind=kOutput, calls=%fused_computation.268 | convolution fusion | flops 8388608 | bytes 9502720 | tf_op jit(solution)/shard_map/cgl,cg->cl/dot_general | solution.py:25
  119.4 8.7 %fusion.18 = f32[2048,1,128]{2,1,0:T(1,128)S(1)} fusion(bf16[2048,16,128]{2,0,1:T(8,128)(2,1)} %get-tuple-element.175, bf16[2048,16,1]{1,0,2:T(8,128)(2,1)S(1)} %get-tuple-element.192), kind=kOutput, calls=%fused_computation.270 | convolution fusion | flops 8388608 | bytes 9502720 | tf_op jit(solution)/shard_map/cgl,cg->cl/dot_general | solution.py:25
  128.2 9.0 %fusion.20 = f32[2048,1,128]{2,1,0:T(1,128)S(1)} fusion(bf16[2048,16,128]{2,0,1:T(8,128)(2,1)} %copy-done.9, bf16[2048,16,1]{1,0,2:T(8,128)(2,1)} %get-tuple-element.186), kind=kOutput, calls=%fused_computation.272 | convolution fusion | flops 8388608 | bytes 9502720 | tf_op jit(solution)/shard_map/cgl,cg->cl/dot_general | solution.py:25
  137.1 9.8 %fusion.22 = f32[2048,1,128]{2,1,0:T(1,128)} fusion(bf16[2048,16,128]{2,0,1:T(8,128)(2,1)} %copy-done.8, bf16[2048,16,1]{1,0,2:T(8,128)(2,1)} %get-tuple-element.187), kind=kOutput, calls=%fused_computation.274 | convolution fusion | flops 8388608 | bytes 9502720 | tf_op jit(solution)/shard_map/cgl,cg->cl/dot_general | solution.py:25
  146.9 10.2 %fusion.24 = f32[2048,1,128]{2,1,0:T(1,128)} fusion(bf16[2048,16,128]{2,0,1:T(8,128)(2,1)} %copy-done.7, bf16[2048,16,1]{1,0,2:T(8,128)(2,1)} %get-tuple-element.188), kind=kOutput, calls=%fused_computation.276 | convolution fusion | flops 8388608 | bytes 9502720 | tf_op jit(solution)/shard_map/cgl,cg->cl/dot_general | solution.py:25
  157.1 9.8 %fusion.26 = f32[2048,1,128]{2,1,0:T(1,128)} fusion(bf16[2048,16,128]{2,0,1:T(8,128)(2,1)} %copy-done.6, bf16[2048,16,1]{1,0,2:T(8,128)(2,1)} %get-tuple-element.189), kind=kOutput, calls=%fused_computation.278 | convolution fusion | flops 8388608 | bytes 9502720 | tf_op jit(solution)/shard_map/cgl,cg->cl/dot_general | solution.py:25
  166.8 9.9 %fusion.30 = f32[2048,1,128]{2,1,0:T(1,128)} fusion(bf16[2048,16,128]{2,0,1:T(8,128)(2,1)} %get-tuple-element.149, bf16[2048,16,1]{1,0,2:T(8,128)(2,1)S(1)} %get-tuple-element.190), kind=kOutput, calls=%fused_computation.282 | convolution fusion | flops 8388608 | bytes 9502720 | tf_op jit(solution)/shard_map/cgl,cg->cl/dot_general | solution.py:25
  176.7 9.8 %fusion.28 = f32[2048,1,128]{2,1,0:T(1,128)} fusion(bf16[2048,16,128]{2,0,1:T(8,128)(2,1)} %get-tuple-element.141, bf16[2048,16,1]{1,0,2:T(8,128)(2,1)S(1)} %get-tuple-element.185), kind=kOutput, calls=%fused_computation.280 | convolution fusion | flops 8388608 | bytes 9502720 | tf_op jit(solution)/shard_map/cgl,cg->cl/dot_general | solution.py:25
  191.4 5.1 %all-to-all-start = ((bf16[8,2,16384]{2,1,0:T(2,128)(2,1)}), bf16[8,2,16384]{2,1,0:T(2,128)(2,1)}, u32[]{:S(2)}, u32[]{:S(2)}) async-start(bf16[8,2,16384]{2,1,0:T(2,128)(2,1)} %reshape.110), calls=%async_computation | async-start | bytes 1048576 | tf_op jit(solution)/shard_map/all_to_all | solution.py:85
  201.5 10.4 %all-to-all-done = bf16[8,2,16384]{2,1,0:T(2,128)(2,1)} async-done(((bf16[8,2,16384]{2,1,0:T(2,128)(2,1)}), bf16[8,2,16384]{2,1,0:T(2,128)(2,1)}, u32[]{:S(2)}, u32[]{:S(2)}) %all-to-all-start) | async-done | bytes 524320 | tf_op jit(solution)/shard_map/all_to_all | solution.py:85
  215.7 3.5 add_bitcast_fusion
  238.0 3.3 multiply_subtract_fusion.1
  241.3 3.6 fusion.34
  244.9 3.6 fusion.32
  248.6 4.0 fusion.73
  252.5 3.8 multiply_subtract_fusion
  263.2 3.7 all-to-all-start.2
  269.6 23.6 %all-to-all-done.2 = bf16[256,8,255]{2,0,1:T(8,128)(2,1)S(1)} async-done(((bf16[256,8,255]{2,0,1:T(8,128)(2,1)}), bf16[256,8,255]{2,0,1:T(8,128)(2,1)S(1)}, u32[]{:S(2)}, u32[]{:S(2)}) %all-to-all-start.2) | async-done | bytes 1044512 | tf_op jit(solution)/shard_map/all_to_all | solution.py:109
  341.4 3.2 copy-done.10
  349.6 9.1 %fusion.14 = f32[2048,1,128]{2,1,0:T(1,128)S(1)} fusion(bf16[2048,16,128]{2,0,1:T(8,128)(2,1)} %get-tuple-element.20, bf16[2048,16,1]{1,0,2:T(8,128)(2,1)S(1)} %copy-done.5), kind=kOutput, calls=%fused_computation.266 | convolution fusion | flops 8388608 | bytes 9502720 | tf_op jit(solution)/shard_map/cgl,cg->cl/dot_general | solution.py:25
  358.7 8.7 %fusion.12 = f32[2048,1,128]{2,1,0:T(1,128)S(1)} fusion(bf16[2048,16,128]{2,0,1:T(8,128)(2,1)} %copy-done.10, bf16[2048,16,1]{1,0,2:T(8,128)(2,1)S(1)} %copy-done.4), kind=kOutput, calls=%fused_computation.264 | convolution fusion | flops 8388608 | bytes 9502720 | tf_op jit(solution)/shard_map/cgl,cg->cl/dot_general | solution.py:25
  367.5 8.9 %fusion.10 = f32[2048,1,128]{2,1,0:T(1,128)S(1)} fusion(bf16[2048,16,128]{2,0,1:T(8,128)(2,1)} %get-tuple-element.19, bf16[2048,16,1]{1,0,2:T(8,128)(2,1)S(1)} %get-tuple-element.181), kind=kOutput, calls=%fused_computation.262 | convolution fusion | flops 8388608 | bytes 9502720 | tf_op jit(solution)/shard_map/cgl,cg->cl/dot_general | solution.py:25
  376.4 8.8 %fusion.8 = f32[2048,1,128]{2,1,0:T(1,128)S(1)} fusion(bf16[2048,16,128]{2,0,1:T(8,128)(2,1)} %get-tuple-element.18, bf16[2048,16,1]{1,0,2:T(8,128)(2,1)} %get-tuple-element.180), kind=kOutput, calls=%fused_computation.260 | convolution fusion | flops 8388608 | bytes 9502720 | tf_op jit(solution)/shard_map/cgl,cg->cl/dot_general | solution.py:25
  385.1 9.9 %fusion.6 = f32[2048,1,128]{2,1,0:T(1,128)} fusion(bf16[2048,16,128]{2,0,1:T(8,128)(2,1)} %get-tuple-element.17, bf16[2048,16,1]{1,0,2:T(8,128)(2,1)} %get-tuple-element.179), kind=kOutput, calls=%fused_computation.258 | convolution fusion | flops 8388608 | bytes 9502720 | tf_op jit(solution)/shard_map/cgl,cg->cl/dot_general | solution.py:25
  395.0 9.8 %fusion.4 = f32[2048,1,128]{2,1,0:T(1,128)} fusion(bf16[2048,16,128]{2,0,1:T(8,128)(2,1)} %get-tuple-element.16, bf16[2048,16,1]{1,0,2:T(8,128)(2,1)} %get-tuple-element.178), kind=kOutput, calls=%fused_computation.256 | convolution fusion | flops 8388608 | bytes 9502720 | tf_op jit(solution)/shard_map/cgl,cg->cl/dot_general | solution.py:25
  404.8 9.7 %fusion.2 = f32[2048,1,128]{2,1,0:T(1,128)} fusion(bf16[2048,16,128]{2,0,1:T(8,128)(2,1)} %copy-done.12, bf16[2048,16,1]{1,0,2:T(8,128)(2,1)S(1)} %get-tuple-element.184), kind=kOutput, calls=%fused_computation.254 | convolution fusion | flops 8388608 | bytes 9502720 | tf_op jit(solution)/shard_map/cgl,cg->cl/dot_general | solution.py:25
  414.5 10.1 %fusion = f32[2048,1,128]{2,1,0:T(1,128)} fusion(bf16[2048,16,128]{2,0,1:T(8,128)(2,1)} %copy-done.11, bf16[2048,16,1]{1,0,2:T(8,128)(2,1)} %get-tuple-element.183), kind=kOutput, calls=%fused_computation.252 | convolution fusion | flops 8388608 | bytes 9502720 | tf_op jit(solution)/shard_map/cgl,cg->cl/dot_general | solution.py:25
  424.5 3.6 multiply_convert_fusion
  (172 shorter events, 186.8 us)
Async XLA Ops:
  0.0 20.0 %copy-start = (bf16[2048,128]{1,0:T(8,128)(2,1)S(1)}, bf16[2048,128]{1,0:T(8,128)(2,1)}, u32[]{:S(2)}) copy-start(bf16[2048,128]{1,0:T(8,128)(2,1)} %param.7) | copy-start | bytes 1572868
  2.1 17.9 %collective-permute-start = (bf16[2048,127]{1,0:T(8,128)(2,1)}, bf16[2048,127]{1,0:T(8,128)(2,1)S(1)}, u32[]{:S(2)}, u32[]{:S(2)}) collective-permute-start(bf16[2048,127]{1,0:T(8,128)(2,1)} %slice.819), channel_id=1, source_target_pairs={{0,2},{2,4},{4,6},{6,8},{8,10},{10,12},{12,14},{1,3},{3,5},{5,7},{... | collective-permute-start | bytes 1560584 | tf_op jit(solution)/shard_map/ppermute | solution.py:11
  8.2 183.2 %all-to-all-start.1 = ((bf16[8,2,16384]{2,1,0:T(2,128)(2,1)}), bf16[8,2,16384]{2,1,0:T(2,128)(2,1)S(1)}, u32[]{:S(2)}, u32[]{:S(2)}) async-start(bf16[8,2,16384]{2,1,0:T(2,128)(2,1)} %reshape.112), calls=%async_computation.1 | async-start | bytes 1048576 | tf_op jit(solution)/shard_map/all_to_all | solution.py:79
  28.0 3.2 copy-start.13
  63.3 5.3 %copy-start.6 = (bf16[2048,16,128]{2,0,1:T(8,128)(2,1)}, bf16[2048,16,128]{2,0,1:T(8,128)(2,1)S(1)}, u32[]{:S(2)}) copy-start(bf16[2048,16,128]{2,0,1:T(8,128)(2,1)S(1)} %get-tuple-element.157) | copy-start | bytes 25165828
  71.9 5.3 %copy-start.7 = (bf16[2048,16,128]{2,0,1:T(8,128)(2,1)}, bf16[2048,16,128]{2,0,1:T(8,128)(2,1)S(1)}, u32[]{:S(2)}) copy-start(bf16[2048,16,128]{2,0,1:T(8,128)(2,1)S(1)} %get-tuple-element.163) | copy-start | bytes 25165828
  79.6 7.1 %copy-start.8 = (bf16[2048,16,128]{2,0,1:T(8,128)(2,1)}, bf16[2048,16,128]{2,0,1:T(8,128)(2,1)S(1)}, u32[]{:S(2)}) copy-start(bf16[2048,16,128]{2,0,1:T(8,128)(2,1)S(1)} %get-tuple-element.168) | copy-start | bytes 25165828
  86.7 14.3 %copy-start.9 = (bf16[2048,16,128]{2,0,1:T(8,128)(2,1)}, bf16[2048,16,128]{2,0,1:T(8,128)(2,1)S(1)}, u32[]{:S(2)}) copy-start(bf16[2048,16,128]{2,0,1:T(8,128)(2,1)S(1)} %get-tuple-element.172) | copy-start | bytes 25165828
  176.7 9.8 %copy-start.2 = (bf16[2048,128]{1,0:T(8,128)(2,1)S(1)}, bf16[2048,128]{1,0:T(8,128)(2,1)}, u32[]{:S(2)}) copy-start(bf16[2048,128]{1,0:T(8,128)(2,1)} %param.8) | copy-start | bytes 1572868
  191.4 20.5 %all-to-all-start = ((bf16[8,2,16384]{2,1,0:T(2,128)(2,1)}), bf16[8,2,16384]{2,1,0:T(2,128)(2,1)}, u32[]{:S(2)}, u32[]{:S(2)}) async-start(bf16[8,2,16384]{2,1,0:T(2,128)(2,1)} %reshape.110), calls=%async_computation | async-start | bytes 1048576 | tf_op jit(solution)/shard_map/all_to_all | solution.py:85
  256.3 10.6 %copy-start.1 = (bf16[2048,128]{1,0:T(8,128)(2,1)S(1)}, bf16[2048,128]{1,0:T(8,128)(2,1)}, u32[]{:S(2)}) copy-start(bf16[2048,128]{1,0:T(8,128)(2,1)} %param.12) | copy-start | bytes 1572868
  263.2 30.1 %all-to-all-start.2 = ((bf16[256,8,255]{2,0,1:T(8,128)(2,1)}), bf16[256,8,255]{2,0,1:T(8,128)(2,1)S(1)}, u32[]{:S(2)}, u32[]{:S(2)}) async-start(bf16[256,8,255]{2,0,1:T(8,128)(2,1)} %copy.106), calls=%async_computation.2 | async-start | bytes 2097152 | tf_op jit(solution)/shard_map/all_to_all | solution.py:109
  335.5 14.1 %copy-start.5 = (bf16[2048,16,1]{1,0,2:T(8,128)(2,1)S(1)}, bf16[2048,16,1]{1,0,2:T(8,128)(2,1)}, u32[]{:S(2)}) copy-start(bf16[2048,16,1]{1,0,2:T(8,128)(2,1)} %get-tuple-element.182) | copy-start | bytes 196612
  341.4 3.2 copy-start.10
  341.4 5.8 %copy-start.11 = (bf16[2048,16,128]{2,0,1:T(8,128)(2,1)}, bf16[2048,16,128]{2,0,1:T(8,128)(2,1)S(1)}, u32[]{:S(2)}) copy-start(bf16[2048,16,128]{2,0,1:T(8,128)(2,1)S(1)} %get-tuple-element.14) | copy-start | bytes 25165828
  341.4 8.2 %copy-start.12 = (bf16[2048,16,128]{2,0,1:T(8,128)(2,1)}, bf16[2048,16,128]{2,0,1:T(8,128)(2,1)S(1)}, u32[]{:S(2)}) copy-start(bf16[2048,16,128]{2,0,1:T(8,128)(2,1)S(1)} %get-tuple-element.15) | copy-start | bytes 25165828
  341.4 17.4 %copy-start.4 = (bf16[2048,16,1]{1,0,2:T(8,128)(2,1)S(1)}, bf16[2048,16,1]{1,0,2:T(8,128)(2,1)}, u32[]{:S(2)}) copy-start(bf16[2048,16,1]{1,0,2:T(8,128)(2,1)} %get-tuple-element.177) | copy-start | bytes 196612
  414.5 10.1 %copy-start.3 = (bf16[2048,128]{1,0:T(8,128)(2,1)S(1)}, bf16[2048,128]{1,0:T(8,128)(2,1)}, u32[]{:S(2)}) copy-start(bf16[2048,128]{1,0:T(8,128)(2,1)} %param.13) | copy-start | bytes 1572868
where the time goes:
time: 436 us; the launch traced here: 429 us
  matrix products  201 us (46%)
  other arithmetic  97.6 us (22%)
  local copies, waits for them, and re-layouts  78 us (18%)
  waiting for transfers between devices  34.1 us (8%)
  starting transfers between devices  17.4 us (4%)
    dot_general x16, matrix products, depthwise(): jnp.einsum('cgl,cg->cl', stacked, kernel_taps[:, first:last], preferred_e...  151 us
    unnamed x91, other arithmetic  67.5 us
    unnamed x49, local copies, waits for them, and re-layouts  62 us
    dot_general x18, matrix products, contract(): return jnp.einsum(form, left, right, precision=lax.Precision.HIGHEST)  50 us
    all_to_all x1, waiting for transfers between devices, on_device(): lax.all_to_all(windows, ('tok', 'sec'), split_axis=1, concat_axis=0, tile...  23.6 us
    another operation x8, other arithmetic, depthwise(): jnp.stack([padded[:, tap_count - 1 - k:tap_count - 1 - k + length] for k...  19.8 us
    all_to_all x1, waiting for transfers between devices, on_device(): lax.all_to_all(mixed_one[:, None, :], ('tok', 'sec'), split_axis=0, conca...  10.4 us
  transfers between devices with their start and end apart: 4, of which 2 were waited for; matrix products, arithmetic and copies ran while one was open for 43% of the time, Pallas kernels for 0%

commit v1 on v0

--- a/solution.py
+++ b/solution.py
@@ -3,6 +3,29 @@
 import jax.numpy as jnp
 from jax import lax
 from jax.sharding import PartitionSpec as P
+
+
+def cut_along(x, dim, size):
+    dims = x.shape
+    pieces = x.reshape(*dims[:dim], size, dims[dim] // size, *dims[dim + 1 :])
+    return jnp.moveaxis(pieces, dim, 0)
+
+
+def laid_out(tiles, dim):
+    lengths = list(tiles.shape[1:])
+    lengths[dim] *= tiles.shape[0]
+    return jnp.moveaxis(tiles, 0, dim).reshape(lengths)
+
+
+def exchange_directly(value, axis, split_dim, concat_dim):
+    length, here = (lax.axis_size(axis), lax.axis_index(axis))
+    blocks = cut_along(value, split_dim, length)
+    gathered = [blocks[here]]
+    for step in range(1, length):
+        sent = blocks[(here + step) % length]
+        gathered.append(lax.ppermute(sent, axis, [(i, (i + step) % length) for i in range(length)]))
+    blocks = jnp.stack(gathered)[(here - jnp.arange(length)) % length]
+    return laid_out(blocks, concat_dim)
 
 
 def passed_along(array, axis, by):
@@ -106,9 +129,9 @@
         axis=1,
     )
     windows = jnp.concatenate([tail_rows, long_blocks], axis=2)
-    padded = lax.all_to_all(
-        windows, ("tok", "sec"), split_axis=1, concat_axis=0, tiled=True
-    ).reshape(channels, block_len + rim_width)
+    padded = exchange_directly(windows, ("tok", "sec"), 1, 0).reshape(
+        channels, block_len + rim_width
+    )
     second_conv = depthwise(padded, taps_two)
     return (second_conv * gate_two).astype(jnp.bfloat16)
 

time: 436 us -> 459 us (1.053)
  the two profiles are of different devices: /device:TPU:0 before, /device:TPU:15 now
where the time goes in v1:
time: 459 us; the launch traced here: 451 us
  matrix products  201 us (44%)
  other arithmetic  97 us (21%)
  local copies, waits for them, and re-layouts  80.4 us (18%)
  waiting for transfers between devices  48.5 us (11%)
  starting transfers between devices  23.4 us (5%)
    dot_general x16, matrix products, depthwise(): jnp.einsum('cgl,cg->cl', stacked, kernel_taps[:, first:last], preferred_e...  151 us
    unnamed x91, other arithmetic  67.1 us
    unnamed x74, local copies, waits for them, and re-layouts  61.7 us
    dot_general x18, matrix products, contract(): return jnp.einsum(form, left, right, precision=lax.Precision.HIGHEST)  50 us
    ppermute x7, waiting for transfers between devices, exchange_directly(): lax.ppermute(sent, axis, [(i, (i + step) % length) for i in range(length)])  41 us
    another operation x8, other arithmetic, depthwise(): jnp.stack([padded[:, tap_count - 1 - k:tap_count - 1 - k + length] for k...  19.7 us
    ppermute x7, starting transfers between devices, exchange_directly(): lax.ppermute(sent, axis, [(i, (i + step) % length) for i in range(length)])  10.5 us
  transfers between devices with their start and end apart: 10, of which 6 were waited for; matrix products, arithmetic and copies ran while one was open for 41% of the time, Pallas kernels for 0%

profile of v1, /device:TPU:15, one launch (start us, length us, event | category | flops | bytes accessed | tf_op | source)
XLA Modules:
  0.0 451.3 jit_solution(11562362181308214435)
XLA Ops:
  2.1 3.8 collective-permute-start
  9.4 4.0 all-to-all-start.1
  13.4 5.7 %slice_bitcast_fusion.142 = (bf16[2048,16,1]{1,0,2:T(8,128)(2,1)}, bf16[2048,16,1]{1,0,2:T(8,128)(2,1)}, bf16[2048,16,1]{1,0,2:T(8,128)(2,1)}, bf16[2048,16,1]{1...) fusion(bf16[2048,128]{1,0:T(8,128)(2,1)} %param.9), kind=kLoop, calls=%fused_computation.1022 | loop fusion | bytes 1048576 | tf_op jit(solution)/shard_map/slice | solution.py:49
  113.1 8.7 %fusion.16 = f32[2048,1,128]{2,1,0:T(1,128)S(1)} fusion(bf16[2048,16,128]{2,0,1:T(8,128)(2,1)} %constant_dynamic-update-slice_fusion.112, bf16[2048,16,1]{1,0,2:T(8,128)(2,1)S(1)} %get-tuple-element.199), kind=kOutput, calls=%fused_computation.269 | convolution fusion | flops 8388608 | bytes 9502720 | tf_op jit(solution)/shard_map/cgl,cg->cl/dot_general | solution.py:48
  121.8 8.8 %fusion.18 = f32[2048,1,128]{2,1,0:T(1,128)S(1)} fusion(bf16[2048,16,128]{2,0,1:T(8,128)(2,1)} %get-tuple-element.183, bf16[2048,16,1]{1,0,2:T(8,128)(2,1)S(1)} %get-tuple-element.200), kind=kOutput, calls=%fused_computation.271 | convolution fusion | flops 8388608 | bytes 9502720 | tf_op jit(solution)/shard_map/cgl,cg->cl/dot_general | solution.py:48
  130.6 9.2 %fusion.20 = f32[2048,1,128]{2,1,0:T(1,128)S(1)} fusion(bf16[2048,16,128]{2,0,1:T(8,128)(2,1)} %copy-done.18, bf16[2048,16,1]{1,0,2:T(8,128)(2,1)S(1)} %copy-done.14), kind=kOutput, calls=%fused_computation.273 | convolution fusion | flops 8388608 | bytes 9502720 | tf_op jit(solution)/shard_map/cgl,cg->cl/dot_general | solution.py:48
  139.8 9.8 %fusion.22 = f32[2048,1,128]{2,1,0:T(1,128)} fusion(bf16[2048,16,128]{2,0,1:T(8,128)(2,1)} %copy-done.17, bf16[2048,16,1]{1,0,2:T(8,128)(2,1)S(1)} %copy-done.13), kind=kOutput, calls=%fused_computation.275 | convolution fusion | flops 8388608 | bytes 9502720 | tf_op jit(solution)/shard_map/cgl,cg->cl/dot_general | solution.py:48
  149.6 10.0 %fusion.24 = f32[2048,1,128]{2,1,0:T(1,128)} fusion(bf16[2048,16,128]{2,0,1:T(8,128)(2,1)} %copy-done.16, bf16[2048,16,1]{1,0,2:T(8,128)(2,1)S(1)} %copy-done.12), kind=kOutput, calls=%fused_computation.277 | convolution fusion | flops 8388608 | bytes 9502720 | tf_op jit(solution)/shard_map/cgl,cg->cl/dot_general | solution.py:48
  159.5 9.8 %fusion.26 = f32[2048,1,128]{2,1,0:T(1,128)} fusion(bf16[2048,16,128]{2,0,1:T(8,128)(2,1)} %copy-done.15, bf16[2048,16,1]{1,0,2:T(8,128)(2,1)S(1)} %copy-done.11), kind=kOutput, calls=%fused_computation.279 | convolution fusion | flops 8388608 | bytes 9502720 | tf_op jit(solution)/shard_map/cgl,cg->cl/dot_general | solution.py:48
  169.3 10.2 %fusion.30 = f32[2048,1,128]{2,1,0:T(1,128)} fusion(bf16[2048,16,128]{2,0,1:T(8,128)(2,1)} %get-tuple-element.157, bf16[2048,16,1]{1,0,2:T(8,128)(2,1)S(1)} %copy-done.10), kind=kOutput, calls=%fused_computation.283 | convolution fusion | flops 8388608 | bytes 9502720 | tf_op jit(solution)/shard_map/cgl,cg->cl/dot_general | solution.py:48
  179.5 9.8 %fusion.28 = f32[2048,1,128]{2,1,0:T(1,128)} fusion(bf16[2048,16,128]{2,0,1:T(8,128)(2,1)} %get-tuple-element.149, bf16[2048,16,1]{1,0,2:T(8,128)(2,1)S(1)} %copy-done.9), kind=kOutput, calls=%fused_computation.281 | convolution fusion | flops 8388608 | bytes 9502720 | tf_op jit(solution)/shard_map/cgl,cg->cl/dot_general | solution.py:48
  194.2 5.1 %all-to-all-start = ((bf16[8,2,16384]{2,1,0:T(2,128)(2,1)}), bf16[8,2,16384]{2,1,0:T(2,128)(2,1)}, u32[]{:S(2)}, u32[]{:S(2)}) async-start(bf16[8,2,16384]{2,1,0:T(2,128)(2,1)} %reshape.197), calls=%async_computation | async-start | bytes 1048576 | tf_op jit(solution)/shard_map/all_to_all | solution.py:108
  203.6 7.5 %all-to-all-done = bf16[8,2,16384]{2,1,0:T(2,128)(2,1)} async-done(((bf16[8,2,16384]{2,1,0:T(2,128)(2,1)}), bf16[8,2,16384]{2,1,0:T(2,128)(2,1)}, u32[]{:S(2)}, u32[]{:S(2)}) %all-to-all-start) | async-done | bytes 524320 | tf_op jit(solution)/shard_map/all_to_all | solution.py:108
  214.7 3.5 add_bitcast_fusion
  237.0 3.5 multiply_subtract_fusion.1
  240.5 3.6 fusion.34
  244.1 3.6 fusion.32
  247.7 3.7 fusion.73
  251.5 3.8 multiply_subtract_fusion
  274.0 3.5 collective-permute-done.2
  277.9 26.8 %collective-permute-done.3 = bf16[256,1,255]{2,1,0:T(2,128)(2,1)S(1)} collective-permute-done((bf16[256,1,255]{2,1,0:T(2,128)(2,1)S(1)}, bf16[256,1,255]{2,1,0:T(2,128)(2,1)S(1)}, u32[]{:S(2)}, u32[]{:S(2)}) %collective-permute-start.3) | collective-permute-done | bytes 130592 | tf_op jit(solution)/shard_map/ppermute | solution.py:26
  304.7 5.6 %collective-permute-done.4 = bf16[256,1,255]{2,1,0:T(2,128)(2,1)S(1)} collective-permute-done((bf16[256,1,255]{2,1,0:T(2,128)(2,1)S(1)}, bf16[256,1,255]{2,1,0:T(2,128)(2,1)S(1)}, u32[]{:S(2)}, u32[]{:S(2)}) %collective-permute-start.4) | collective-permute-done | bytes 130592 | tf_op jit(solution)/shard_map/ppermute | solution.py:26
  310.4 5.0 %collective-permute-done.6 = bf16[256,1,255]{2,1,0:T(2,128)(2,1)S(1)} collective-permute-done((bf16[256,1,255]{2,1,0:T(2,128)(2,1)S(1)}, bf16[256,1,255]{2,1,0:T(2,128)(2,1)S(1)}, u32[]{:S(2)}, u32[]{:S(2)}) %collective-permute-start.6) | collective-permute-done | bytes 130592 | tf_op jit(solution)/shard_map/ppermute | solution.py:26
  372.3 8.9 %fusion.14 = f32[2048,1,128]{2,1,0:T(1,128)S(1)} fusion(bf16[2048,16,128]{2,0,1:T(8,128)(2,1)} %get-tuple-element.20, bf16[2048,16,1]{1,0,2:T(8,128)(2,1)S(1)} %copy-done.8), kind=kOutput, calls=%fused_computation.267 | convolution fusion | flops 8388608 | bytes 9502720 | tf_op jit(solution)/shard_map/cgl,cg->cl/dot_general | solution.py:48
  381.3 8.8 %fusion.12 = f32[2048,1,128]{2,1,0:T(1,128)S(1)} fusion(bf16[2048,16,128]{2,0,1:T(8,128)(2,1)} %copy-done.19, bf16[2048,16,1]{1,0,2:T(8,128)(2,1)S(1)} %copy-done.7), kind=kOutput, calls=%fused_computation.265 | convolution fusion | flops 8388608 | bytes 9502720 | tf_op jit(solution)/shard_map/cgl,cg->cl/dot_general | solution.py:48
  390.0 9.1 %fusion.10 = f32[2048,1,128]{2,1,0:T(1,128)S(1)} fusion(bf16[2048,16,128]{2,0,1:T(8,128)(2,1)} %get-tuple-element.19, bf16[2048,16,1]{1,0,2:T(8,128)(2,1)S(1)} %copy-done.6), kind=kOutput, calls=%fused_computation.263 | convolution fusion | flops 8388608 | bytes 9502720 | tf_op jit(solution)/shard_map/cgl,cg->cl/dot_general | solution.py:48
  399.2 8.8 %fusion.8 = f32[2048,1,128]{2,1,0:T(1,128)S(1)} fusion(bf16[2048,16,128]{2,0,1:T(8,128)(2,1)} %get-tuple-element.18, bf16[2048,16,1]{1,0,2:T(8,128)(2,1)} %get-tuple-element.188), kind=kOutput, calls=%fused_computation.261 | convolution fusion | flops 8388608 | bytes 9502720 | tf_op jit(solution)/shard_map/cgl,cg->cl/dot_general | solution.py:48
  408.0 9.7 %fusion.6 = f32[2048,1,128]{2,1,0:T(1,128)} fusion(bf16[2048,16,128]{2,0,1:T(8,128)(2,1)} %get-tuple-element.17, bf16[2048,16,1]{1,0,2:T(8,128)(2,1)S(1)} %copy-done.5), kind=kOutput, calls=%fused_computation.259 | convolution fusion | flops 8388608 | bytes 9502720 | tf_op jit(solution)/shard_map/cgl,cg->cl/dot_general | solution.py:48
  417.7 10.0 %fusion.4 = f32[2048,1,128]{2,1,0:T(1,128)} fusion(bf16[2048,16,128]{2,0,1:T(8,128)(2,1)} %get-tuple-element.16, bf16[2048,16,1]{1,0,2:T(8,128)(2,1)} %get-tuple-element.186), kind=kOutput, calls=%fused_computation.257 | convolution fusion | flops 8388608 | bytes 9502720 | tf_op jit(solution)/shard_map/cgl,cg->cl/dot_general | solution.py:48
  427.7 9.7 %fusion.2 = f32[2048,1,128]{2,1,0:T(1,128)} fusion(bf16[2048,16,128]{2,0,1:T(8,128)(2,1)} %copy-done.21, bf16[2048,16,1]{1,0,2:T(8,128)(2,1)S(1)} %copy-done.4), kind=kOutput, calls=%fused_computation.255 | convolution fusion | flops 8388608 | bytes 9502720 | tf_op jit(solution)/shard_map/cgl,cg->cl/dot_general | solution.py:48
  437.4 10.0 %fusion = f32[2048,1,128]{2,1,0:T(1,128)} fusion(bf16[2048,16,128]{2,0,1:T(8,128)(2,1)} %copy-done.20, bf16[2048,16,1]{1,0,2:T(8,128)(2,1)} %get-tuple-element.191), kind=kOutput, calls=%fused_computation.253 | convolution fusion | flops 8388608 | bytes 9502720 | tf_op jit(solution)/shard_map/cgl,cg->cl/dot_general | solution.py:48
  447.5 3.6 multiply_convert_fusion
  (213 shorter events, 206.9 us)
Async XLA Ops:
  0.0 19.9 %copy-start.1 = (bf16[2048,128]{1,0:T(8,128)(2,1)S(1)}, bf16[2048,128]{1,0:T(8,128)(2,1)}, u32[]{:S(2)}) copy-start(bf16[2048,128]{1,0:T(8,128)(2,1)} %param.12) | copy-start | bytes 1572868
  2.1 20.8 %collective-permute-start = (bf16[2048,127]{1,0:T(8,128)(2,1)}, bf16[2048,127]{1,0:T(8,128)(2,1)S(1)}, u32[]{:S(2)}, u32[]{:S(2)}) collective-permute-start(bf16[2048,127]{1,0:T(8,128)(2,1)} %slice.819), channel_id=1, source_target_pairs={{0,2},{2,4},{4,6},{6,8},{8,10},{10,12},{12,14},{1,3},{3,5},{5,7},{... | collective-permute-start | bytes 1560584 | tf_op jit(solution)/shard_map/ppermute | solution.py:34
  9.4 184.8 %all-to-all-start.1 = ((bf16[8,2,16384]{2,1,0:T(2,128)(2,1)}), bf16[8,2,16384]{2,1,0:T(2,128)(2,1)S(1)}, u32[]{:S(2)}, u32[]{:S(2)}) async-start(bf16[8,2,16384]{2,1,0:T(2,128)(2,1)} %reshape.199), calls=%async_computation.1 | async-start | bytes 1048576 | tf_op jit(solution)/shard_map/all_to_all | solution.py:102
  13.4 9.5 %copy-start = (bf16[2048,128]{1,0:T(8,128)(2,1)S(1)}, bf16[2048,128]{1,0:T(8,128)(2,1)}, u32[]{:S(2)}) copy-start(bf16[2048,128]{1,0:T(8,128)(2,1)} %param.7) | copy-start | bytes 1572868
  65.9 5.3 %copy-start.15 = (bf16[2048,16,128]{2,0,1:T(8,128)(2,1)}, bf16[2048,16,128]{2,0,1:T(8,128)(2,1)S(1)}, u32[]{:S(2)}) copy-start(bf16[2048,16,128]{2,0,1:T(8,128)(2,1)S(1)} %get-tuple-element.165) | copy-start | bytes 25165828
  74.6 5.3 %copy-start.16 = (bf16[2048,16,128]{2,0,1:T(8,128)(2,1)}, bf16[2048,16,128]{2,0,1:T(8,128)(2,1)S(1)}, u32[]{:S(2)}) copy-start(bf16[2048,16,128]{2,0,1:T(8,128)(2,1)S(1)} %get-tuple-element.171) | copy-start | bytes 25165828
  82.2 7.1 %copy-start.17 = (bf16[2048,16,128]{2,0,1:T(8,128)(2,1)}, bf16[2048,16,128]{2,0,1:T(8,128)(2,1)S(1)}, u32[]{:S(2)}) copy-start(bf16[2048,16,128]{2,0,1:T(8,128)(2,1)S(1)} %get-tuple-element.176) | copy-start | bytes 25165828
  89.3 14.2 %copy-start.18 = (bf16[2048,16,128]{2,0,1:T(8,128)(2,1)}, bf16[2048,16,128]{2,0,1:T(8,128)(2,1)S(1)}, u32[]{:S(2)}) copy-start(bf16[2048,16,128]{2,0,1:T(8,128)(2,1)S(1)} %get-tuple-element.180) | copy-start | bytes 25165828
  121.8 8.8 %copy-start.14 = (bf16[2048,16,1]{1,0,2:T(8,128)(2,1)S(1)}, bf16[2048,16,1]{1,0,2:T(8,128)(2,1)}, u32[]{:S(2)}) copy-start(bf16[2048,16,1]{1,0,2:T(8,128)(2,1)} %get-tuple-element.194) | copy-start | bytes 196612
  130.6 9.2 %copy-start.13 = (bf16[2048,16,1]{1,0,2:T(8,128)(2,1)S(1)}, bf16[2048,16,1]{1,0,2:T(8,128)(2,1)}, u32[]{:S(2)}) copy-start(bf16[2048,16,1]{1,0,2:T(8,128)(2,1)} %get-tuple-element.195) | copy-start | bytes 196612
  139.8 9.8 %copy-start.12 = (bf16[2048,16,1]{1,0,2:T(8,128)(2,1)S(1)}, bf16[2048,16,1]{1,0,2:T(8,128)(2,1)}, u32[]{:S(2)}) copy-start(bf16[2048,16,1]{1,0,2:T(8,128)(2,1)} %get-tuple-element.196) | copy-start | bytes 196612
  149.5 10.0 %copy-start.11 = (bf16[2048,16,1]{1,0,2:T(8,128)(2,1)S(1)}, bf16[2048,16,1]{1,0,2:T(8,128)(2,1)}, u32[]{:S(2)}) copy-start(bf16[2048,16,1]{1,0,2:T(8,128)(2,1)} %get-tuple-element.197) | copy-start | bytes 196612
  159.5 9.8 %copy-start.10 = (bf16[2048,16,1]{1,0,2:T(8,128)(2,1)S(1)}, bf16[2048,16,1]{1,0,2:T(8,128)(2,1)}, u32[]{:S(2)}) copy-start(bf16[2048,16,1]{1,0,2:T(8,128)(2,1)} %get-tuple-element.198) | copy-start | bytes 196612
  169.3 10.2 %copy-start.9 = (bf16[2048,16,1]{1,0,2:T(8,128)(2,1)S(1)}, bf16[2048,16,1]{1,0,2:T(8,128)(2,1)}, u32[]{:S(2)}) copy-start(bf16[2048,16,1]{1,0,2:T(8,128)(2,1)} %get-tuple-element.193) | copy-start | bytes 196612
  179.5 9.8 %copy-start.2 = (bf16[2048,128]{1,0:T(8,128)(2,1)S(1)}, bf16[2048,128]{1,0:T(8,128)(2,1)}, u32[]{:S(2)}) copy-start(bf16[2048,128]{1,0:T(8,128)(2,1)} %param.8) | copy-start | bytes 1572868
  194.2 16.9 %all-to-all-start = ((bf16[8,2,16384]{2,1,0:T(2,128)(2,1)}), bf16[8,2,16384]{2,1,0:T(2,128)(2,1)}, u32[]{:S(2)}, u32[]{:S(2)}) async-start(bf16[8,2,16384]{2,1,0:T(2,128)(2,1)} %reshape.197), calls=%async_computation | async-start | bytes 1048576 | tf_op jit(solution)/shard_map/all_to_all | solution.py:108
  263.8 7.8 %collective-permute-start.1 = (bf16[256,1,255]{2,1,0:T(2,128)(2,1)S(1)}, bf16[256,1,255]{2,1,0:T(2,128)(2,1)S(1)}, u32[]{:S(2)}, u32[]{:S(2)}) collective-permute-start(bf16[256,1,255]{2,1,0:T(2,128)(2,1)S(1)} %get-tuple-element.147), channel_id=1, source_target_pairs={{0,2},{2,4},{4,6},{6,8},{8,10},{10,12},{12,14},{14,0},{1,3},{3,5},... | collective-permute-start | bytes 391688 | tf_op jit(solution)/shard_map/ppermute | solution.py:26
  265.5 12.0 %collective-permute-start.2 = (bf16[256,1,255]{2,1,0:T(2,128)(2,1)S(1)}, bf16[256,1,255]{2,1,0:T(2,128)(2,1)S(1)}, u32[]{:S(2)}, u32[]{:S(2)}) collective-permute-start(bf16[256,1,255]{2,1,0:T(2,128)(2,1)S(1)} %get-tuple-element.146), channel_id=1, source_target_pairs={{0,4},{2,6},{4,8},{6,10},{8,12},{10,14},{12,0},{14,2},{1,5},{3,7},... | collective-permute-start | bytes 391688 | tf_op jit(solution)/shard_map/ppermute | solution.py:26
  267.5 37.2 %collective-permute-start.3 = (bf16[256,1,255]{2,1,0:T(2,128)(2,1)S(1)}, bf16[256,1,255]{2,1,0:T(2,128)(2,1)S(1)}, u32[]{:S(2)}, u32[]{:S(2)}) collective-permute-start(bf16[256,1,255]{2,1,0:T(2,128)(2,1)S(1)} %get-tuple-element.145), channel_id=1, source_target_pairs={{0,6},{2,8},{4,10},{6,12},{8,14},{10,0},{12,2},{14,4},{1,7},{3,9},... | collective-permute-start | bytes 391688 | tf_op jit(solution)/shard_map/ppermute | solution.py:26
  269.9 40.5 %collective-permute-start.4 = (bf16[256,1,255]{2,1,0:T(2,128)(2,1)S(1)}, bf16[256,1,255]{2,1,0:T(2,128)(2,1)S(1)}, u32[]{:S(2)}, u32[]{:S(2)}) collective-permute-start(bf16[256,1,255]{2,1,0:T(2,128)(2,1)S(1)} %get-tuple-element.144), channel_id=1, source_target_pairs={{0,8},{2,10},{4,12},{6,14},{8,0},{10,2},{12,4},{14,6},{1,9},{3,11}... | collective-permute-start | bytes 391688 | tf_op jit(solution)/shard_map/ppermute | solution.py:26
  269.9 40.5 %collective-permute-start.5 = (bf16[256,1,255]{2,1,0:T(2,128)(2,1)S(1)}, bf16[256,1,255]{2,1,0:T(2,128)(2,1)S(1)}, u32[]{:S(2)}, u32[]{:S(2)}) collective-permute-start(bf16[256,1,255]{2,1,0:T(2,128)(2,1)S(1)} %get-tuple-element.143), channel_id=1, source_target_pairs={{0,10},{2,12},{4,14},{6,0},{8,2},{10,4},{12,6},{14,8},{1,11},{3,13... | collective-permute-start | bytes 391688 | tf_op jit(solution)/shard_map/ppermute | solution.py:26
  271.6 43.8 %collective-permute-start.6 = (bf16[256,1,255]{2,1,0:T(2,128)(2,1)S(1)}, bf16[256,1,255]{2,1,0:T(2,128)(2,1)S(1)}, u32[]{:S(2)}, u32[]{:S(2)}) collective-permute-start(bf16[256,1,255]{2,1,0:T(2,128)(2,1)S(1)} %get-tuple-element.142), channel_id=1, source_target_pairs={{0,12},{2,14},{4,0},{6,2},{8,4},{10,6},{12,8},{14,10},{1,13},{3,15... | collective-permute-start | bytes 391688 | tf_op jit(solution)/shard_map/ppermute | solution.py:26
  277.5 37.9 %collective-permute-start.7 = (bf16[256,1,255]{2,1,0:T(2,128)(2,1)S(1)}, bf16[256,1,255]{2,1,0:T(2,128)(2,1)S(1)}, u32[]{:S(2)}, u32[]{:S(2)}) collective-permute-start(bf16[256,1,255]{2,1,0:T(2,128)(2,1)S(1)} %get-tuple-element.141), channel_id=1, source_target_pairs={{0,14},{2,0},{4,2},{6,4},{8,6},{10,8},{12,10},{14,12},{1,15},{3,1}... | collective-permute-start | bytes 391688 | tf_op jit(solution)/shard_map/ppermute | solution.py:26
  358.1 14.2 %copy-start.8 = (bf16[2048,16,1]{1,0,2:T(8,128)(2,1)S(1)}, bf16[2048,16,1]{1,0,2:T(8,128)(2,1)}, u32[]{:S(2)}) copy-start(bf16[2048,16,1]{1,0,2:T(8,128)(2,1)} %get-tuple-element.190) | copy-start | bytes 196612
  364.0 3.2 copy-start.19
  364.0 5.8 %copy-start.20 = (bf16[2048,16,128]{2,0,1:T(8,128)(2,1)}, bf16[2048,16,128]{2,0,1:T(8,128)(2,1)S(1)}, u32[]{:S(2)}) copy-start(bf16[2048,16,128]{2,0,1:T(8,128)(2,1)S(1)} %get-tuple-element.14) | copy-start | bytes 25165828
  364.0 8.3 %copy-start.21 = (bf16[2048,16,128]{2,0,1:T(8,128)(2,1)}, bf16[2048,16,128]{2,0,1:T(8,128)(2,1)S(1)}, u32[]{:S(2)}) copy-start(bf16[2048,16,128]{2,0,1:T(8,128)(2,1)S(1)} %get-tuple-element.15) | copy-start | bytes 25165828
  364.0 17.2 %copy-start.7 = (bf16[2048,16,1]{1,0,2:T(8,128)(2,1)S(1)}, bf16[2048,16,1]{1,0,2:T(8,128)(2,1)}, u32[]{:S(2)}) copy-start(bf16[2048,16,1]{1,0,2:T(8,128)(2,1)} %get-tuple-element.185) | copy-start | bytes 196612
  381.2 8.8 %copy-start.6 = (bf16[2048,16,1]{1,0,2:T(8,128)(2,1)S(1)}, bf16[2048,16,1]{1,0,2:T(8,128)(2,1)}, u32[]{:S(2)}) copy-start(bf16[2048,16,1]{1,0,2:T(8,128)(2,1)} %get-tuple-element.189) | copy-start | bytes 196612
  399.2 8.8 %copy-start.5 = (bf16[2048,16,1]{1,0,2:T(8,128)(2,1)S(1)}, bf16[2048,16,1]{1,0,2:T(8,128)(2,1)}, u32[]{:S(2)}) copy-start(bf16[2048,16,1]{1,0,2:T(8,128)(2,1)} %get-tuple-element.187) | copy-start | bytes 196612
  417.7 10.0 %copy-start.4 = (bf16[2048,16,1]{1,0,2:T(8,128)(2,1)S(1)}, bf16[2048,16,1]{1,0,2:T(8,128)(2,1)}, u32[]{:S(2)}) copy-start(bf16[2048,16,1]{1,0,2:T(8,128)(2,1)} %get-tuple-element.192) | copy-start | bytes 196612
  437.4 10.0 %copy-start.3 = (bf16[2048,128]{1,0:T(8,128)(2,1)S(1)}, bf16[2048,128]{1,0:T(8,128)(2,1)}, u32[]{:S(2)}) copy-start(bf16[2048,128]{1,0:T(8,128)(2,1)} %param.13) | copy-start | bytes 1572868
  (1 other events, 3.2 us)
